TPU v7x, 256 devices: a whole 4x4x8 slice. The times are simulated.
256 devices in a mesh: walk: 128 (over x, z, y), tan: 2 (over core).
Axes of the slice: x: 4, y: 4, z: 8, core: 2. Of those that a mesh axis runs over, the one named last changes fastest.
Arguments:
- values: bfloat16 [512, 64, 256], P('walk', 'tan'), may hold values from -6 to 6
- lap_in: bfloat16 [512, 64, 256], P('walk', 'tan'), may hold values from -6 to 6
- tangent: bfloat16 [512, 192, 64, 256], P('walk', None, 'tan'), may hold values from -0.4375 to 0.4375
- slot_electron: int32 [512, 64], P('walk'), may hold values from 0 to 63, each once within a row
- spin_up: int32 [512], P('walk'), may hold values from 16 to 48
- w_self: bfloat16 [256, 256], replicated, may hold values from -0.375 to 0.375
- w_spin: bfloat16 [256, 256], replicated, may hold values from -1.5 to 1.5
- bias: float32 [256], replicated, may hold values from -3 to 3
- readout: float32 [256], replicated, may hold values from -0.046875 to 0.046875
- potential: float32 [512], P('walk'), may hold values from -6 to 6
Outputs:
- laplacian: float32 [512, 64, 256], P('walk', 'tan')
- energy: float32 [512], P('walk')
- grad_self: float32 [256, 256], replicated
- grad_spin: float32 [256, 256], replicated
Inputs may be any that keep to these rules, and one draw needn't show every extreme that they name: `slot_electron`: each walker's row names every electron once.
All inputs are finite; a program needn't handle non-finite values.
Results may differ from a plain program's by a relative error of at most 0.004.
Values may be sent and summed in bfloat16 or wider, within the bound.
A program may use at most 64 MiB of HBM per device.

v0:
```python
import jax
import jax.numpy as jnp
from jax import lax
from jax.sharding import PartitionSpec as P


def pick_spin(upper_spin, mixed_rows):
    return (
        upper_spin[..., :, None] * mixed_rows[..., 0:1, :]
        + (1.0 - upper_spin[..., :, None]) * mixed_rows[..., 1:2, :]
    )


def shards(
    values, lap_in, tangent, slot_electron, spin_up, w_self, w_spin, bias, readout, potential
):
    tan_rank = lax.axis_index("tan")
    walkers, own_slots, feat_width = values.shape
    electrons = slot_electron.shape[1]
    first_slot = tan_rank * own_slots

    def own_slice(array_in, axis_dim):
        return lax.dynamic_slice_in_dim(array_in, first_slot, own_slots, axis_dim)

    full_values, full_lap = (
        lax.all_gather(values, "tan", axis=1, tiled=True),
        lax.all_gather(lap_in, "tan", axis=1, tiled=True),
    )
    upper_spin = (slot_electron < spin_up[:, None]).astype(jnp.float32)
    mask_rows = jnp.stack([upper_spin, 1.0 - upper_spin], axis=1)
    mask_bf = mask_rows.astype(jnp.bfloat16)
    up_count = spin_up.astype(jnp.float32)
    count_rows = jnp.stack([up_count, electrons - up_count], axis=1)

    def group_mean(field):
        group_sums = jnp.einsum("wse,wef->wsf", mask_bf, field, preferred_element_type=jnp.float32)
        return (group_sums / count_rows[:, :, None]).astype(jnp.bfloat16)

    mean_values = group_mean(full_values)
    mean_lap = group_mean(full_lap)
    mix_values = jnp.einsum("wsf,fg->wsg", mean_values, w_spin, preferred_element_type=jnp.float32)
    mix_lap = jnp.einsum("wsf,fg->wsg", mean_lap, w_spin, preferred_element_type=jnp.float32)
    preact = (
        jnp.einsum("wef,fg->weg", full_values, w_self, preferred_element_type=jnp.float32)
        + pick_spin(upper_spin, mix_values)
        + bias
    )
    lap_pre = jnp.einsum(
        "wef,fg->weg", full_lap, w_self, preferred_element_type=jnp.float32
    ) + pick_spin(upper_spin, mix_lap)
    squash = jnp.tanh(preact)
    slopes = 1.0 - squash * squash
    curvature = -2.0 * squash * slopes
    weighted_slope = slopes * readout
    own_upper = own_slice(upper_spin, 1)
    own_weighted = own_slice(weighted_slope, 1)
    own_mask = own_slice(mask_bf, 2)
    partial_sums = jnp.einsum(
        "wse,wdef->wdsf", own_mask, tangent, preferred_element_type=jnp.float32
    )
    spin_sums = lax.psum(partial_sums, "tan")
    spin_means = (spin_sums / count_rows[:, None, :, None]).astype(jnp.bfloat16)
    mixed_all = jnp.einsum("wdsf,fg->wdsg", spin_means, w_spin, preferred_element_type=jnp.float32)

    def per_walker(walker_items):
        tangent_block, mixed_rows, upper_row, slope_row = walker_items
        change = jnp.dot(
            tangent_block.reshape(-1, feat_width), w_self, preferred_element_type=jnp.float32
        ).reshape(tangent_block.shape) + pick_spin(upper_row, mixed_rows)
        squares = jnp.sum(change * change, axis=0)
        grad_rows = jnp.einsum("def,ef->d", change, slope_row, precision=lax.Precision.HIGHEST)
        return (squares, grad_rows)

    own_squares, partial_grad = lax.map(per_walker, (tangent, mixed_all, own_upper, own_weighted))
    laplacian = own_slice(slopes, 1) * own_slice(lap_pre, 1) + own_slice(curvature, 1) * own_squares
    lap_total, gradient = lax.psum((jnp.sum(laplacian * readout, axis=(1, 2)), partial_grad), "tan")
    grad_total = jnp.sum(gradient * gradient, axis=1)
    energy = -0.5 * (lap_total + grad_total) + potential
    slope_bf = own_weighted.astype(jnp.bfloat16)
    picked = pick_spin(own_upper, mean_values.astype(jnp.float32)).astype(jnp.bfloat16)
    first_terms = jnp.einsum("wef,weg->wfg", values, slope_bf, preferred_element_type=jnp.float32)
    spin_terms = jnp.einsum("wef,weg->wfg", picked, slope_bf, preferred_element_type=jnp.float32)
    all_walkers = walkers * lax.axis_size("walk")
    center = lax.psum(jnp.sum(energy), "walk") / all_walkers
    spread = energy - center
    grad_self, grad_spin = lax.psum(
        (
            jnp.einsum("w,wfg->fg", spread, first_terms, precision=lax.Precision.HIGHEST),
            jnp.einsum("w,wfg->fg", spread, spin_terms, precision=lax.Precision.HIGHEST),
        ),
        ("walk", "tan"),
    )
    return (laplacian, energy, grad_self, grad_spin)


def solution(mesh):
    placed = (
        P("walk", "tan", None),
        P("walk", "tan", None),
        P("walk", None, "tan", None),
        P("walk", None),
        P("walk"),
        P(),
        P(),
        P(),
        P(),
        P("walk"),
    )
    return jax.shard_map(
        shards,
        mesh=mesh,
        in_specs=placed,
        out_specs=(P("walk", "tan", None), P("walk"), P(), P()),
        check_vma=False,
    )
```

profile of v0, /device:TPU:1, one launch (start us, length us, event | category | flops | bytes accessed | tf_op | source)
XLA Modules:
  0.0 725.8 jit_solution(9727683264933580680)
XLA Ops:
  7.2 0.8 broadcast_subtract_fusion.2
  8.1 6.5 fusion.42
  14.6 1.3 copy.65
  16.1 4.7 all_gather.6
  21.8 2.1 all_gather.7
  25.4 1.2 fusion.33
  26.6 25.2 %all-reduce.5.cloned.1.call-done = f32[4,192,2,256]{3,1,2,0:T(8,128)} async-done(((f32[4,192,2,256]{3,1,2,0:T(8,128)}), f32[4,192,2,256]{3,1,2,0:T(8,128)}) %all-reduce.5.cloned.1.call-update) | async-done | bytes 1572880 | tf_op jit(solution)/shard_map/psum | solution.py:61
  51.7 3.0 fusion.20
  54.7 55.3 %while.12 = (s32[]{:T(128)}, f32[4,32,256]{2,1,0:T(8,128)S(1)}, f32[4,192]{1,0:T(4,128)}, bf16[4,192,32,256]{3,2,1,0:T(8,128)(2,1)}, bf16[256,256]{1,0:T(8,128)(...) while((s32[]{:T(128)}, f32[4,32,256]{2,1,0:T(8,128)S(1)}, ...), condition=%wide.region_3.4_spmd, body=%wide.region_1.3_spmd.sunk | while | flops 833609792 | bytes 18025972 | solution.py:74
  54.7 1.0 dynamic-slice_bitcast_fusion.3
  55.8 3.5 multiply_reduce_fusion.4
  59.3 7.9 %fusion.72 = f32[1,192]{1,0:T(1,128)S(1)} fusion(f32[192,32,256]{2,1,0:T(8,128)S(1)} %get-tuple-element.161, f32[32,256,1]{1,0,2:T(8,128)S(1)} %get-tuple-element.162), kind=kOutput, calls=%fused_computation.7.clone.1 | convolution fusion | flops 18874368 | bytes 6324992 | tf_op jit(solution)/shard_map/while/body/eval_jaxpr/def,ef->d/dot_general | solution.py:71
  67.3 1.3 dynamic_update_slice.12
  68.6 1.0 dynamic-slice_bitcast_fusion.3
  69.7 3.5 multiply_reduce_fusion.4
  73.2 7.9 %fusion.72 = f32[1,192]{1,0:T(1,128)S(1)} fusion(f32[192,32,256]{2,1,0:T(8,128)S(1)} %get-tuple-element.161, f32[32,256,1]{1,0,2:T(8,128)S(1)} %get-tuple-element.162), kind=kOutput, calls=%fused_computation.7.clone.1 | convolution fusion | flops 18874368 | bytes 6324992 | tf_op jit(solution)/shard_map/while/body/eval_jaxpr/def,ef->d/dot_general | solution.py:71
  81.1 1.3 dynamic_update_slice.12
  82.4 1.0 dynamic-slice_bitcast_fusion.3
  83.5 3.5 multiply_reduce_fusion.4
  87.0 7.9 %fusion.72 = f32[1,192]{1,0:T(1,128)S(1)} fusion(f32[192,32,256]{2,1,0:T(8,128)S(1)} %get-tuple-element.161, f32[32,256,1]{1,0,2:T(8,128)S(1)} %get-tuple-element.162), kind=kOutput, calls=%fused_computation.7.clone.1 | convolution fusion | flops 18874368 | bytes 6324992 | tf_op jit(solution)/shard_map/while/body/eval_jaxpr/def,ef->d/dot_general | solution.py:71
  94.9 1.3 dynamic_update_slice.12
  96.2 1.0 dynamic-slice_bitcast_fusion.3
  97.3 3.5 multiply_reduce_fusion.4
  100.8 7.9 %fusion.72 = f32[1,192]{1,0:T(1,128)S(1)} fusion(f32[192,32,256]{2,1,0:T(8,128)S(1)} %get-tuple-element.161, f32[32,256,1]{1,0,2:T(8,128)S(1)} %get-tuple-element.162), kind=kOutput, calls=%fused_computation.7.clone.1 | convolution fusion | flops 18874368 | bytes 6324992 | tf_op jit(solution)/shard_map/while/body/eval_jaxpr/def,ef->d/dot_general | solution.py:71
  108.8 1.3 dynamic_update_slice.12
  110.8 2.6 all-reduce.1
  114.2 295.3 %psum.45 = f32[]{:T(128)} all-reduce(f32[]{:T(128)} %get-tuple-element.73), channel_id=1, replica_groups=mesh['walk'=128,'tan'=2] {'walk'}, use_global_device_ids=true, to_apply=%region_9.10 | all-reduce | flops 1 | bytes 8 | tf_op jit(solution)/shard_map/psum | solution.py:84
  410.2 2.3 fusion.18
  413.2 1.8 fusion.49
  415.8 299.9 %all-reduce.7.cloned.1.call-done = (f32[256,256]{1,0:T(8,128)}, f32[256,256]{1,0:T(8,128)}) async-done(((f32[256,256]{1,0:T(8,128)}, f32[256,256]{1,0:T(8,128)}), (f32[256,256]{1,0:T(8,128)}, f32[256,256]{1,0:T(8,128)})) %all-reduce.7.cloned.1.call-update) | async-done | bytes 524304 | tf_op jit(solution)/shard_map/psum | solution.py:86
  715.7 1.7 copy.86
  717.3 1.7 copy.87
  (66 shorter events, 5.8 us)
Async XLA Ops:
  7.2 13.8 %copy-start = (bf16[256,256]{1,0:T(8,128)(2,1)S(1)}, bf16[256,256]{1,0:T(8,128)(2,1)}, u32[]{:S(2)}) copy-start(bf16[256,256]{1,0:T(8,128)(2,1)} %param.18) | copy-start | bytes 393220
  7.2 44.6 %all-reduce.5.cloned.1.call-start = ((), (), s32[]{:S(2)}) async-start(), calls=%async_computation | async-start | bytes 3145728 | tf_op jit(solution)/shard_map/psum | solution.py:61
  8.0 7.9 %copy-start.10 = (s32[4]{0:T(128)S(1)}, s32[4]{0:T(128)}, u32[]{:S(2)}) copy-start(s32[4]{0:T(128)} %param.16) | copy-start | bytes 52
  8.1 8.1 %copy-start.2 = (bf16[4,32,256]{2,1,0:T(8,128)(2,1)S(1)}, bf16[4,32,256]{2,1,0:T(8,128)(2,1)}, u32[]{:S(2)}) copy-start(bf16[4,32,256]{2,1,0:T(8,128)(2,1)} %param.12) | copy-start | bytes 196612
  8.1 13.7 %copy-start.3 = (bf16[4,32,256]{2,1,0:T(8,128)(2,1)S(1)}, bf16[4,32,256]{2,1,0:T(8,128)(2,1)}, u32[]{:S(2)}) copy-start(bf16[4,32,256]{2,1,0:T(8,128)(2,1)} %param.13) | copy-start | bytes 196612
  8.1 15.8 %copy-start.1 = (bf16[256,256]{1,0:T(8,128)(2,1)S(1)}, bf16[256,256]{1,0:T(8,128)(2,1)}, u32[]{:S(2)}) copy-start(bf16[256,256]{1,0:T(8,128)(2,1)} %param.17) | copy-start | bytes 393220
  8.1 15.8 %copy-start.8 = (f32[256]{0:T(256)S(1)}, f32[256]{0:T(256)}, u32[]{:S(2)}) copy-start(f32[256]{0:T(256)} %param.19) | copy-start | bytes 3076
  14.6 9.5 %copy-start.5 = (f32[256]{0:T(256)S(1)}, f32[256]{0:T(256)}, u32[]{:S(2)}) copy-start(f32[256]{0:T(256)} %param.20) | copy-start | bytes 3076
  15.9 699.8 %all-reduce.7.cloned.1.call-start = ((), (), s32[]{:S(2)}) async-start(), calls=%async_computation.1 | async-start | bytes 1048576 | tf_op jit(solution)/shard_map/psum | solution.py:86
  16.1 8.9 %copy-start.7 = (f32[4,2]{1,0:T(4,128)}, f32[4,2]{1,0:T(4,128)S(1)}, u32[]{:S(2)}) copy-start(f32[4,2]{1,0:T(4,128)S(1)} %copy.33) | copy-start | bytes 100
  54.7 55.3 %copy-start.6 = (f32[256]{0:T(256)S(1)}, f32[256]{0:T(256)}, u32[]{:S(2)}) copy-start(f32[256]{0:T(256)} %param.20) | copy-start | bytes 3076
  54.7 58.8 %copy-start.9 = (f32[4]{0:T(128)S(1)}, f32[4]{0:T(128)}, u32[]{:S(2)}) copy-start(f32[4]{0:T(128)} %param.21) | copy-start | bytes 52
  114.2 604.8 %copy-start.4 = (f32[4]{0:T(128)}, f32[4]{0:T(128)S(1)}, u32[]{:S(2)}) copy-start(f32[4]{0:T(128)S(1)} %get-tuple-element.194) | copy-start | bytes 52
Sparse Core Ops, SparseCore 0:
  16.0 35.6 all-reduce.4
  415.9 299.7 all-reduce.6
where the time goes:
time: 727 us; the launch traced here: 726 us
  waiting for transfers between devices  325 us (45%)
  blocking collectives  305 us (42%)
  matrix products  61.7 us (8%)
  local copies, waits for them, and re-layouts  16.2 us (2%)
  between operations  14.9 us (2%)
    psum x1, waiting for transfers between devices, shards(): lax.psum((jnp.einsum('w,wfg->fg', spread, first_terms, precision=lax.Prec...  300 us
    psum x1, blocking collectives, shards(): center = lax.psum(jnp.sum(energy), 'walk') / all_walkers  295 us
    dot_general x4, matrix products, per_walker(): jnp.einsum('def,ef->d', change, slope_row, precision=lax.Precision.HIGHEST)  31.7 us
    psum x1, waiting for transfers between devices, shards(): spin_sums = lax.psum(partial_sums, 'tan')  25.2 us
  transfers between devices with their start and end apart: 2, of which 2 were waited for; matrix products, arithmetic and copies ran while one was open for 1% of the time, Pallas kernels for 0%

commit v1 on v0

v1 whole, which is shorter than its diff:
```python
import jax
import jax.numpy as jnp
from jax import lax
from jax.experimental import pallas as pl
from jax.experimental.pallas import tpu as pltpu
from jax.sharding import PartitionSpec as P

MESH = pl.DeviceIdType.MESH
F32 = jnp.float32
BF16 = jnp.bfloat16
NX, NZ, NY = 4, 8, 4
XY = NX * NY
BLOCK = 8


def iota(shape, axis):
    return lax.broadcasted_iota(jnp.int32, shape, axis)


def dot(a, b):
    return jnp.dot(a, b, preferred_element_type=F32)


def body(
    values, lap_in, tangent, slots, spin, w_self, w_spin, bias, readout, potential,
    lap_out, energy_out, grads_out,
    full_v, full_l, tan, own_sums, got_sums, mixed, sel, terms, slopes_s, lap_pre_s,
    partial, own_ex, got_ex, shard_s, recv_s, mine_s, zs, shard_e, recv_e, mine_e, ze,
    load_sem, tan_sem, pair_send, pair_recv,
    rs_send, rs_recv, z_send, z_recv, ag_send, ag_recv,
):
    walkers, dirs, own, feat = tangent.shape
    elec = slots.shape[1]
    rows = BLOCK * own
    blocks = dirs // BLOCK
    me = lax.axis_index("walk")
    core = lax.axis_index("tan")
    x = me // (NZ * NY)
    z = (me // NY) % NZ
    y = me % NY
    here = x * NY + y
    partner = (me, 1 - core)

    def across(k):
        px = (x + k // NY) % NX
        py = (y + k % NY) % NY
        return (px * NZ + z) * NY + py, px * NY + py

    def behind(k):
        return ((x - k // NY + NX) % NX) * NY + (y - k % NY + NY) % NY

    def along(k):
        return (x * NZ + (z + k) % NZ) * NY + y

    off = pl.multiple_of(core * own, own)
    load_v = pltpu.make_async_copy(values, full_v.at[:, pl.ds(off, own)], load_sem.at[0])
    load_l = pltpu.make_async_copy(lap_in, full_l.at[:, pl.ds(off, own)], load_sem.at[1])
    for w in range(walkers):
        pltpu.make_async_copy(tangent.at[w], tan.at[w], tan_sem.at[w]).start()
        if w == 0:
            load_v.start()
            load_l.start()

    barrier = pltpu.get_barrier_semaphore()
    pl.semaphore_signal(barrier, inc=1, device_id=partner, device_id_type=MESH)

    def greet(k, carry):
        to, _ = across(k)
        for other in (core, 1 - core):
            pl.semaphore_signal(barrier, inc=1, device_id=(to, other), device_id_type=MESH)
        return carry

    def greet_z(k, carry):
        pl.semaphore_signal(barrier, inc=1, device_id=(along(k), core), device_id_type=MESH)
        return carry

    lax.fori_loop(1, XY, greet, 0)
    lax.fori_loop(1, NZ, greet_z, 0)

    s8 = jnp.concatenate([slots[...]] * (8 // walkers), 0)
    r8 = iota((8, elec), 0) % walkers
    n8 = jnp.zeros((8, elec), jnp.int32)
    for w in range(walkers):
        n8 = jnp.where(r8 == w, spin[w], n8)
    upper = (s8 < n8).astype(F32).astype(BF16)
    spread = (iota((elec, rows), 0) == core * own + iota((elec, rows), 1) % own).astype(F32)
    tiled = dot(upper, spread.astype(BF16))
    eye = (iota((elec, elec), 0) == iota((elec, elec), 1)).astype(F32).astype(BF16)
    columns = lax.dot_general(eye, upper, (((1,), (1,)), ((), ())), preferred_element_type=F32)
    own_eye = (iota((own, elec), 0) + core * own == iota((own, elec), 1)).astype(F32).astype(BF16)
    own_columns = lax.dot_general(
        own_eye, upper, (((1,), (1,)), ((), ())), preferred_element_type=F32
    )
    r16 = iota((2 * BLOCK, rows), 0)
    c16 = iota((2 * BLOCK, rows), 1)
    for w in range(walkers):
        m = tiled[w : w + 1]
        m = jnp.where(r16 < BLOCK, m, 1.0 - m)
        sel[w] = jnp.where(c16 // own == r16 % BLOCK, m, 0.0).astype(BF16)

    def group_sums(w):
        pick = sel[w]

        def step(i, carry):
            d = pl.multiple_of(i * BLOCK, BLOCK)
            t = tan[w, pl.ds(d, BLOCK)].reshape(rows, feat)
            r = dot(pick, t)
            own_sums[w, 0, pl.ds(d, BLOCK)] = r[:BLOCK]
            own_sums[w, 1, pl.ds(d, BLOCK)] = r[BLOCK:]
            return carry

        lax.fori_loop(0, blocks, step, 0, unroll=4)

    def sums_copy(w):
        return pltpu.make_async_remote_copy(
            src_ref=own_sums.at[w],
            dst_ref=got_sums.at[w],
            send_sem=pair_send.at[w],
            recv_sem=pair_recv.at[w],
            device_id=partner,
            device_id_type=MESH,
        )

    def tan_wait(w):
        pltpu.make_async_copy(tangent.at[w], tan.at[w], tan_sem.at[w]).wait()

    tan_wait(0)
    group_sums(0)
    pl.semaphore_wait(barrier, 1 + 2 * (XY - 1) + NZ - 1)

    def to_partner(src, dst, i):
        return pltpu.make_async_remote_copy(
            src_ref=src,
            dst_ref=dst,
            send_sem=pair_send.at[i],
            recv_sem=pair_recv.at[i],
            device_id=partner,
            device_id_type=MESH,
        )

    send_v = to_partner(values, full_v.at[:, pl.ds(off, own)], walkers)
    send_l = to_partner(lap_in, full_l.at[:, pl.ds(off, own)], walkers + 1)
    send_v.start()
    send_l.start()
    sums_copy(0).start()
    for w in range(1, walkers):
        tan_wait(w)
        group_sums(w)
        sums_copy(w).start()
    load_v.wait()
    load_l.wait()
    send_v.wait()
    send_l.wait()

    gain = readout[...].reshape(1, feat)
    shift = bias[...].reshape(1, feat)
    row8 = iota((8, elec), 0)
    row81 = iota((8, 1), 0)
    total = jnp.zeros((feat, feat), F32)
    for w in range(walkers):
        n0 = spin[w].astype(F32)
        n1 = elec - n0
        up = upper[w : w + 1].astype(F32)
        masks = jnp.where(row8 == 0, up, jnp.where(row8 == 1, 1.0 - up, 0.0)).astype(BF16)
        counts = jnp.where(row81 == 0, n0, jnp.where(row81 == 1, n1, 1.0))
        mean_v = (dot(masks, full_v[w]) / counts).astype(BF16)
        mean_l = (dot(masks, full_l[w]) / counts).astype(BF16)
        mix_v = dot(mean_v, w_spin[...])
        mix_l = dot(mean_l, w_spin[...])
        is_up = columns[:, w : w + 1] > 0.5
        own_up = own_columns[:, w : w + 1] > 0.5
        pre = dot(full_v[w], w_self[...]) + jnp.where(is_up, mix_v[0:1], mix_v[1:2]) + shift
        squash = jnp.tanh(pre)
        slopes = 1.0 - squash * squash
        slopes_s[0, w] = slopes
        slopes_s[1, w] = -2.0 * squash * slopes
        lap_own = full_l[w, pl.ds(off, own)]
        lap_pre_s[w] = dot(lap_own, w_self[...]) + jnp.where(own_up, mix_l[0:1], mix_l[1:2])
        slope_bf = (slopes * gain).astype(BF16)
        mean_f = mean_v.astype(F32)
        picked = jnp.where(is_up, mean_f[0:1], mean_f[1:2])
        left = jnp.where(core == 0, full_v[w].astype(F32), picked).astype(BF16)
        term = lax.dot_general(
            left, slope_bf, (((0,), (0,)), ((), ())), preferred_element_type=F32
        )
        terms[w] = term
        total = total + term
    per = feat // XY
    shard_s[...] = total.reshape(XY, per, feat)

    def scatter(src, dst, send, recv):
        dst[here] = src[here]

        def go(k, carry):
            to, slot = across(k)
            pltpu.make_async_remote_copy(
                src_ref=src.at[slot],
                dst_ref=dst.at[here],
                send_sem=send.at[k],
                recv_sem=recv.at[k],
                device_id=(to, core),
                device_id_type=MESH,
            ).start()
            return carry

        lax.fori_loop(1, XY, go, 0)

    def scatter_wait(src, dst, send, recv):
        def go(k, carry):
            to, slot = across(k)
            pltpu.make_async_remote_copy(
                src_ref=src.at[slot],
                dst_ref=dst.at[behind(k)],
                send_sem=send.at[k],
                recv_sem=recv.at[k],
                device_id=(to, core),
                device_id_type=MESH,
            ).wait()
            return carry

        lax.fori_loop(1, XY, go, 0)

    def over_z(src, dst, send, recv):
        dst[z] = src[...]
        for k in range(1, NZ):
            pltpu.make_async_remote_copy(
                src_ref=src,
                dst_ref=dst.at[z],
                send_sem=send.at[k],
                recv_sem=recv.at[k],
                device_id=(along(k), core),
                device_id_type=MESH,
            ).start()

    def over_z_wait(src, dst, send, recv):
        for k in range(1, NZ):
            pltpu.make_async_remote_copy(
                src_ref=src,
                dst_ref=dst.at[(z - k + NZ) % NZ],
                send_sem=send.at[k],
                recv_sem=recv.at[k],
                device_id=(along(k), core),
                device_id_type=MESH,
            ).wait()

    def add_up(ref, n):
        acc = ref[0]
        for j in range(1, n):
            acc = acc + ref[j]
        return acc

    scatter(shard_s, recv_s, rs_send.at[0], rs_recv.at[0])

    partial[dirs + 1 : dirs + 8] = jnp.zeros((7, 8, 128), F32)
    ones = jnp.ones((8, 128), F32)
    own_ex[...] = jnp.zeros((8, 256), F32)
    for w in range(walkers):
        sums_copy(w).wait()
        n0 = spin[w].astype(F32)
        inv = 1.0 / jnp.concatenate(
            [jnp.full((1, 1, 1), n0, F32), jnp.full((1, 1, 1), elec - n0, F32)], 0
        )
        means = ((own_sums[w] + got_sums[w]) * inv).astype(BF16)
        mixed[...] = dot(means.reshape(2 * dirs, feat), w_spin[...]).reshape(2, dirs, feat)
        own_up = jnp.broadcast_to(own_columns[:, w : w + 1], (own, feat)) > 0.5
        own_slopes = slopes_s[0, w, pl.ds(off, own)]
        own_curve = slopes_s[1, w, pl.ds(off, own)]
        weighted = own_slopes * gain

        def step(i, acc):
            d = pl.multiple_of(i * BLOCK, BLOCK)
            t = tan[w, pl.ds(d, BLOCK)].reshape(rows, feat)
            a = dot(t, w_self[...])
            for j in range(BLOCK):
                m0 = mixed[0, pl.ds(d + j, 1)]
                m1 = mixed[1, pl.ds(d + j, 1)]
                ch = a[j * own : (j + 1) * own] + jnp.where(own_up, m0, m1)
                acc = acc + ch * ch
                p = (ch * weighted).reshape(own // 8, 8, feat).sum(axis=0)
                partial[d + j] = p[:, :128] + p[:, 128:]
            return acc

        squares = lax.fori_loop(0, blocks, step, jnp.zeros((own, feat), F32))
        lap = own_slopes * lap_pre_s[w] + own_curve * squares
        lap_out[w] = lap
        lp = (lap * gain).reshape(own // 8, 8, feat).sum(axis=0)
        partial[dirs] = lp[:, :128] + lp[:, 128:]
        g = jnp.concatenate(
            [partial[...].sum(axis=1), jnp.zeros((256 - dirs - 8, 128), F32)], 0
        )
        g = lax.dot_general(
            ones, g, (((1,), (1,)), ((), ())),
            precision=lax.Precision.HIGHEST, preferred_element_type=F32,
        )
        own_ex[...] = jnp.where(iota((8, 256), 0) == w, g, own_ex[...])
        if w == 1:
            scatter_wait(shard_s, recv_s, rs_send.at[0], rs_recv.at[0])
            mine_s[...] = add_up(recv_s, XY)
            over_z(mine_s, zs, z_send.at[0], z_recv.at[0])

    ex = to_partner(own_ex, got_ex, walkers + 2)
    ex.start()
    ex.wait()
    both = own_ex[...] + got_ex[...]
    lane = iota((8, 256), 1)
    both = jnp.where(lane < dirs, both * both, jnp.where(lane == dirs, both, 0.0))
    pot = jnp.zeros((8, 1), F32)
    for w in range(walkers):
        pot = jnp.where(row81 == w, potential[w], pot)
    energy = -0.5 * jnp.sum(both, axis=1, keepdims=True) + pot
    energy_out[...] = jnp.broadcast_to(energy, (8, 128))
    esum = jnp.broadcast_to(jnp.sum(energy, axis=0, keepdims=True), (8, feat))

    grad = energy[0:1] * terms[0]
    for w in range(1, walkers):
        grad = grad + energy[w : w + 1] * terms[w]
    shard_e[:, :per] = grad.reshape(XY, per, feat)
    shard_e[:, per:] = jnp.broadcast_to(esum[None], (XY, 8, feat))
    scatter(shard_e, recv_e, rs_send.at[1], rs_recv.at[1])
    over_z_wait(mine_s, zs, z_send.at[0], z_recv.at[0])
    plain = add_up(zs, NZ)
    scatter_wait(shard_e, recv_e, rs_send.at[1], rs_recv.at[1])
    mine_e[...] = add_up(recv_e, XY)
    over_z(mine_e, ze, z_send.at[1], z_recv.at[1])
    over_z_wait(mine_e, ze, z_send.at[1], z_recv.at[1])
    summed = add_up(ze, NZ)
    center = summed[per : per + 1] / (walkers * NX * NY * NZ)
    grads_out[core, here] = (summed[:per] - center * plain).astype(BF16)

    def gather_copy(k, other, matrix, slot, i):
        to, _ = across(k)
        return pltpu.make_async_remote_copy(
            src_ref=grads_out.at[core, here],
            dst_ref=grads_out.at[matrix, slot],
            send_sem=ag_send.at[i, k],
            recv_sem=ag_recv.at[i, k],
            device_id=(to, other),
            device_id_type=MESH,
        )

    def gather(k, carry):
        gather_copy(k, core, core, here, 0).start()
        gather_copy(k, 1 - core, core, here, 1).start()
        return carry

    def gather_wait(k, carry):
        gather_copy(k, core, core, behind(k), 0).wait()
        gather_copy(k, 1 - core, 1 - core, behind(k), 1).wait()
        return carry

    gather_copy(0, 1 - core, core, here, 1).start()
    lax.fori_loop(1, XY, gather, 0)
    gather_copy(0, 1 - core, 1 - core, here, 1).wait()
    lax.fori_loop(1, XY, gather_wait, 0)


def shards(
    values, lap_in, tangent, slot_electron, spin_up, w_self, w_spin, bias, readout, potential
):
    walkers, dirs, own, feat = tangent.shape
    elec = slot_electron.shape[1]
    per = feat // XY
    vmem = pl.BlockSpec(memory_space=pltpu.VMEM)
    smem = pl.BlockSpec(memory_space=pltpu.SMEM)
    hbm = pl.BlockSpec(memory_space=pl.ANY)
    dma = pltpu.SemaphoreType.DMA
    lap, energy, grads = pl.pallas_call(
        body,
        out_shape=(
            jax.ShapeDtypeStruct((walkers, own, feat), F32),
            jax.ShapeDtypeStruct((8, 128), F32),
            jax.ShapeDtypeStruct((2, XY, per, feat), BF16),
        ),
        in_specs=[hbm, hbm, hbm, vmem, smem, vmem, vmem, vmem, vmem, smem],
        out_specs=(vmem, vmem, vmem),
        scratch_shapes=[
            pltpu.VMEM((walkers, elec, feat), BF16),
            pltpu.VMEM((walkers, elec, feat), BF16),
            pltpu.VMEM((walkers, dirs, own, feat), BF16),
            pltpu.VMEM((walkers, 2, dirs, feat), F32),
            pltpu.VMEM((walkers, 2, dirs, feat), F32),
            pltpu.VMEM((2, dirs, feat), F32),
            pltpu.VMEM((walkers, 2 * BLOCK, BLOCK * own), BF16),
            pltpu.VMEM((walkers, feat, feat), F32),
            pltpu.VMEM((2, walkers, elec, feat), F32),
            pltpu.VMEM((walkers, own, feat), F32),
            pltpu.VMEM((dirs + 8, 8, 128), F32),
            pltpu.VMEM((8, 256), F32),
            pltpu.VMEM((8, 256), F32),
            pltpu.VMEM((XY, per, feat), F32),
            pltpu.VMEM((XY, per, feat), F32),
            pltpu.VMEM((per, feat), F32),
            pltpu.VMEM((NZ, per, feat), F32),
            pltpu.VMEM((XY, per + 8, feat), F32),
            pltpu.VMEM((XY, per + 8, feat), F32),
            pltpu.VMEM((per + 8, feat), F32),
            pltpu.VMEM((NZ, per + 8, feat), F32),
            dma((2,)),
            dma((walkers,)),
            dma((walkers + 3,)),
            dma((walkers + 3,)),
            dma((2, XY)),
            dma((2, XY)),
            dma((2, NZ)),
            dma((2, NZ)),
            dma((2, XY)),
            dma((2, XY)),
        ],
        compiler_params=pltpu.CompilerParams(
            collective_id=0, has_side_effects=True, vmem_limit_bytes=60 << 20
        ),
        name="forward_laplacian",
    )(values, lap_in, tangent, slot_electron, spin_up, w_self, w_spin, bias, readout, potential)
    grads = grads.astype(F32).reshape(2, feat, feat)
    return lap, energy[:walkers, 0], grads[0], grads[1]


def solution(mesh):
    placed = (
        P("walk", "tan", None),
        P("walk", "tan", None),
        P("walk", None, "tan", None),
        P("walk", None),
        P("walk"),
        P(),
        P(),
        P(),
        P(),
        P("walk"),
    )
    return jax.shard_map(
        shards,
        mesh=mesh,
        in_specs=placed,
        out_specs=(P("walk", "tan", None), P("walk"), P(), P()),
        check_vma=False,
    )
```

time: 727 us -> 69.8 us (0.10)
  waiting for transfers between devices: 325 us -> 0 us
  blocking collectives: 305 us -> 0 us
  Pallas kernels: 0 us -> 64.3 us
  matrix products: 61.7 us -> 0 us
  between operations: 14.9 us -> 0.64 us
  local copies, waits for them, and re-layouts: 16.2 us -> 4.68 us
    psum x2 -> x0, waiting for transfers between devices: 325 us -> none  [the longest x1 300 us: shards(): lax.psum((jnp.einsum('w,wfg->fg', spread, first_terms, precision=lax.Prec...]
    psum x2 -> x0, blocking collectives: 298 us -> none  [the longest x1 295 us: shards(): center = lax.psum(jnp.sum(energy), 'walk') / all_walkers]
    pallas_call x0 -> x1, Pallas kernels: none -> 64.3 us  [shards(): pl.pallas_call(body, out_shape=(jax.ShapeDtypeStruct((walkers, own, feat)...]
    dot_general x20 -> x0, matrix products: 61.7 us -> none  [the longest x4 31.7 us: per_walker(): jnp.einsum('def,ef->d', change, slope_row, precision=lax.Precision.HIGHEST)]
  transfers between devices with their start and end apart: 2 -> 0, of which waited for: 2 -> 0; matrix products, arithmetic and copies ran while one was open for 1% -> 0% of each run, Pallas kernels for 0% -> 0%
where the time goes in v1:
time: 69.8 us; the launch traced here: 69.6 us
  Pallas kernels  64.3 us (92%)
  local copies, waits for them, and re-layouts  4.68 us (7%)
    pallas_call x1, Pallas kernels, shards(): pl.pallas_call(body, out_shape=(jax.ShapeDtypeStruct((walkers, own, feat)...  64.3 us
    slice x2, local copies, waits for them, and re-layouts, shards(): return (lap, energy[:walkers, 0], grads[0], grads[1])  3.11 us
    unnamed x1, local copies, waits for them, and re-layouts  1.57 us

profile of v1, /device:TPU:1, one launch (start us, length us, event | category | flops | bytes accessed | tf_op | source)
XLA Modules:
  0.0 69.6 jit_solution(4880358642489828179)
XLA Ops:
  0.6 64.3 %forward_laplacian.1 = (f32[4,32,256]{2,1,0:T(8,128)}, f32[8,128]{1,0:T(8,128)}, bf16[2,16,16,256]{3,2,1,0:T(8,128)(2,1)}) custom-call(bf16[4,32,256]{2,1,0:T(8,128)(2,1)} %values.1, bf16[4,32,256]{2,1,0:T(8,128)(2,1)} %lap_in.1, bf16[4,192,32,256]{3,2,1,0:T(8,128)(2,1)} %tangent.1, s32[4,64]{1,0:T(4,128)} %slots.1, s32[4]{0:T(128)} %spin.1, ...), custom_call_target="tpu_custom_call" | custom-call | tf_op jit(solution)/shard_map/forward_laplacian/pallas_call | solution.py:367
  64.9 1.3 %slice_reduce_fusion = f32[4]{0:T(128)} fusion(f32[8,128]{1,0:T(8,128)} %get-tuple-element.8), kind=kLoop, calls=%fused_computation | loop fusion | bytes 32 | tf_op jit(solution)/shard_map/slice | solution.py:415
  66.2 1.8 %fusion = (f32[1,16,16,256]{3,2,1,0:T(8,128)}, f32[1,16,16,256]{3,2,1,0:T(8,128)}) fusion(bf16[2,16,16,256]{3,2,1,0:T(8,128)(2,1)} %get-tuple-element.9), kind=kLoop, calls=%fused_computation.1 | loop fusion | bytes 1048576 | tf_op jit(solution)/shard_map/slice | solution.py:415
  68.0 1.6 %copy.15 = f32[4,32,256]{2,1,0:T(8,128)} copy(f32[4,32,256]{2,1,0:T(8,128)} %get-tuple-element.16) | data formatting | bytes 262144

commit v2 on v1

v2 whole, which is shorter than its diff:
```python
import jax
import jax.numpy as jnp
from jax import lax
from jax.experimental import pallas as pl
from jax.experimental.pallas import tpu as pltpu
from jax.sharding import PartitionSpec as P

MESH = pl.DeviceIdType.MESH
F32 = jnp.float32
BF16 = jnp.bfloat16
NX, NZ, NY = 4, 8, 4
XY = NX * NY
BLOCK = 8
STAGE = 32


def iota(shape, axis):
    return lax.broadcasted_iota(jnp.int32, shape, axis)


def dot(a, b):
    return jnp.dot(a, b, preferred_element_type=F32)


def body(
    values, lap_in, tangent, slots, spin, w_self, w_spin, bias, readout, potential,
    lap_out, energy_out, grads_out,
    full_v, full_l, tan, own_sums, got_sums, mixed, sel, terms, slopes_s, lap_pre_s,
    partial, prod_a, prod_b, part_a, part_b, own_ex, got_ex, shard_s, recv_s, mine_s, zs, shard_e, recv_e, mine_e, ze,
    own_e, plane_e, mine_z, all_e,
    load_sem, tan_sem, pair_send, pair_recv,
    rs_send, rs_recv, z_send, z_recv, ag_send, ag_recv,
):
    walkers, dirs, own, feat = tangent.shape
    elec = slots.shape[1]
    rows = BLOCK * own
    blocks = dirs // BLOCK
    me = lax.axis_index("walk")
    core = lax.axis_index("tan")
    x = lax.div(me, NZ * NY)
    z = lax.rem(lax.div(me, NY), NZ)
    y = lax.rem(me, NY)
    here = x * NY + y
    partner = (me, 1 - core)
    xs = [x] + [lax.rem(x + i, NX) for i in range(1, NX)]
    ys = [y] + [lax.rem(y + i, NY) for i in range(1, NY)]
    lines = [xs[i] * (NZ * NY) + z * NY for i in range(NX)]
    columns_z = [me] + [x * (NZ * NY) + lax.rem(z + i, NZ) * NY + y for i in range(1, NZ)]

    def across(k):
        return lines[k // NY] + ys[k % NY], xs[k // NY] * NY + ys[k % NY]

    def behind(k):
        return xs[-(k // NY) % NX] * NY + ys[-(k % NY) % NY]

    def along(k):
        return columns_z[k]

    off = pl.multiple_of(core * own, own)
    load_v = pltpu.make_async_copy(values, full_v.at[:, pl.ds(off, own)], load_sem.at[0])
    load_l = pltpu.make_async_copy(lap_in, full_l.at[:, pl.ds(off, own)], load_sem.at[1])
    for w in range(walkers):
        pltpu.make_async_copy(tangent.at[w], tan.at[w], tan_sem.at[w]).start()
        if w == 0:
            load_v.start()
            load_l.start()

    barrier = pltpu.get_barrier_semaphore()
    pl.semaphore_signal(barrier, inc=1, device_id=partner, device_id_type=MESH)

    for k in range(1, XY):
        for other in (core, 1 - core):
            pl.semaphore_signal(
                barrier, inc=1, device_id=(across(k)[0], other), device_id_type=MESH
            )
    for k in range(1, NZ):
        pl.semaphore_signal(barrier, inc=1, device_id=(along(k), core), device_id_type=MESH)

    s8 = jnp.concatenate([slots[...]] * (8 // walkers), 0)
    r8 = iota((8, elec), 0) % walkers
    n8 = jnp.zeros((8, elec), jnp.int32)
    for w in range(walkers):
        n8 = jnp.where(r8 == w, spin[w], n8)
    upper = (s8 < n8).astype(F32).astype(BF16)
    spread = (iota((elec, rows), 0) == core * own + iota((elec, rows), 1) % own).astype(F32)
    tiled = dot(upper, spread.astype(BF16))
    eye = (iota((elec, elec), 0) == iota((elec, elec), 1)).astype(F32).astype(BF16)
    columns = lax.dot_general(eye, upper, (((1,), (1,)), ((), ())), preferred_element_type=F32)
    own_eye = (iota((own, elec), 0) + core * own == iota((own, elec), 1)).astype(F32).astype(BF16)
    own_columns = lax.dot_general(
        own_eye, upper, (((1,), (1,)), ((), ())), preferred_element_type=F32
    )
    r16 = iota((2 * BLOCK, rows), 0)
    c16 = iota((2 * BLOCK, rows), 1)
    for w in range(walkers):
        m = tiled[w : w + 1]
        m = jnp.where(r16 < BLOCK, m, 1.0 - m)
        sel[w] = jnp.where(c16 // own == r16 % BLOCK, m, 0.0).astype(BF16)

    def group_sums(w):
        pick = sel[w]

        def step(i, carry):
            d = pl.multiple_of(i * BLOCK, BLOCK)
            t = tan[w, pl.ds(d, BLOCK)].reshape(rows, feat)
            r = dot(pick, t)
            own_sums[w, 0, pl.ds(d, BLOCK)] = r[:BLOCK]
            own_sums[w, 1, pl.ds(d, BLOCK)] = r[BLOCK:]
            return carry

        lax.fori_loop(0, blocks, step, 0, unroll=4)

    def sums_copy(w):
        return pltpu.make_async_remote_copy(
            src_ref=own_sums.at[w],
            dst_ref=got_sums.at[w],
            send_sem=pair_send.at[w],
            recv_sem=pair_recv.at[w],
            device_id=partner,
            device_id_type=MESH,
        )

    def tan_wait(w):
        pltpu.make_async_copy(tangent.at[w], tan.at[w], tan_sem.at[w]).wait()

    ahead = 2
    tan_wait(0)
    group_sums(0)
    pl.semaphore_wait(barrier, 1 + 2 * (XY - 1) + NZ - 1)

    def to_partner(src, dst, i):
        return pltpu.make_async_remote_copy(
            src_ref=src,
            dst_ref=dst,
            send_sem=pair_send.at[i],
            recv_sem=pair_recv.at[i],
            device_id=partner,
            device_id_type=MESH,
        )

    send_v = to_partner(values, full_v.at[:, pl.ds(off, own)], walkers)
    send_l = to_partner(lap_in, full_l.at[:, pl.ds(off, own)], walkers + 1)
    send_v.start()
    send_l.start()
    sums_copy(0).start()
    for w in range(1, ahead):
        tan_wait(w)
        group_sums(w)
        sums_copy(w).start()
    load_v.wait()
    load_l.wait()
    send_v.wait()
    send_l.wait()

    gain = readout[...].reshape(1, feat)
    shift = bias[...].reshape(1, feat)
    row8 = iota((8, elec), 0)
    row81 = iota((8, 1), 0)
    total = jnp.zeros((feat, feat), F32)
    for w in range(walkers):
        n0 = spin[w].astype(F32)
        n1 = elec - n0
        up = upper[w : w + 1].astype(F32)
        masks = jnp.where(row8 == 0, up, jnp.where(row8 == 1, 1.0 - up, 0.0)).astype(BF16)
        counts = jnp.where(row81 == 0, n0, jnp.where(row81 == 1, n1, 1.0))
        mean_v = (dot(masks, full_v[w]) / counts).astype(BF16)
        mean_l = (dot(masks, full_l[w]) / counts).astype(BF16)
        mix_v = dot(mean_v, w_spin[...])
        mix_l = dot(mean_l, w_spin[...])
        is_up = columns[:, w : w + 1] > 0.5
        own_up = own_columns[:, w : w + 1] > 0.5
        pre = dot(full_v[w], w_self[...]) + jnp.where(is_up, mix_v[0:1], mix_v[1:2]) + shift
        squash = jnp.tanh(pre)
        slopes = 1.0 - squash * squash
        slopes_s[0, w] = slopes
        slopes_s[1, w] = -2.0 * squash * slopes
        lap_own = full_l[w, pl.ds(off, own)]
        lap_pre_s[w] = dot(lap_own, w_self[...]) + jnp.where(own_up, mix_l[0:1], mix_l[1:2])
        slope_bf = (slopes * gain).astype(BF16)
        mean_f = mean_v.astype(F32)
        picked = jnp.where(is_up, mean_f[0:1], mean_f[1:2])
        left = jnp.where(core == 0, full_v[w].astype(F32), picked).astype(BF16)
        term = lax.dot_general(
            left, slope_bf, (((0,), (0,)), ((), ())), preferred_element_type=F32
        )
        terms[w] = term.reshape(XY, 2, 8, feat)
        total = total + term
    shard_s[...] = total.reshape(shard_s.shape)

    def scatter(src, dst, i, whole=False):
        dst[here] = src[...] if whole else src[here]

        for k in range(1, XY):
            to, slot = across(k)
            pltpu.make_async_remote_copy(
                src_ref=src if whole else src.at[slot],
                dst_ref=dst.at[here],
                send_sem=rs_send.at[i, k],
                recv_sem=rs_recv.at[i, k],
                device_id=(to, core),
                device_id_type=MESH,
            ).start()

    def scatter_wait(src, dst, i, whole=False):
        for k in range(1, XY):
            to, slot = across(k)
            pltpu.make_async_remote_copy(
                src_ref=src if whole else src.at[slot],
                dst_ref=dst.at[behind(k)],
                send_sem=rs_send.at[i, k],
                recv_sem=rs_recv.at[i, k],
                device_id=(to, core),
                device_id_type=MESH,
            ).wait()

    def over_z(src, dst, i):
        dst[z] = src[...]
        for k in range(1, NZ):
            pltpu.make_async_remote_copy(
                src_ref=src,
                dst_ref=dst.at[z],
                send_sem=z_send.at[i, k],
                recv_sem=z_recv.at[i, k],
                device_id=(along(k), core),
                device_id_type=MESH,
            ).start()

    def over_z_wait(src, dst, i):
        for k in range(1, NZ):
            pltpu.make_async_remote_copy(
                src_ref=src,
                dst_ref=dst.at[lax.rem(z - k + NZ, NZ)],
                send_sem=z_send.at[i, k],
                recv_sem=z_recv.at[i, k],
                device_id=(along(k), core),
                device_id_type=MESH,
            ).wait()

    def add_up(ref, n):
        acc = ref[0]
        for j in range(1, n):
            acc = acc + ref[j]
        return acc

    scatter(shard_s, recv_s, 0)

    ones = jnp.ones((8, 128), F32)
    own_ex[...] = jnp.zeros((8, 256), F32)
    partial[dirs:] = jnp.zeros((256 - dirs, 128), F32)
    for w in range(walkers):
        if w + ahead < walkers:
            tan_wait(w + ahead)
            group_sums(w + ahead)
            sums_copy(w + ahead).start()
        sums_copy(w).wait()
        n0 = spin[w].astype(F32)
        inv = 1.0 / jnp.concatenate(
            [jnp.full((1, 1, 1), n0, F32), jnp.full((1, 1, 1), elec - n0, F32)], 0
        )
        means = ((own_sums[w] + got_sums[w]) * inv).astype(BF16)
        mixed[...] = dot(means.reshape(2 * dirs, feat), w_spin[...]).reshape(2, dirs, feat)
        own_up = jnp.broadcast_to(own_columns[:, w : w + 1], (own, feat)) > 0.5
        own_slopes = slopes_s[0, w, pl.ds(off, own)]
        own_curve = slopes_s[1, w, pl.ds(off, own)]
        weighted = own_slopes * gain

        def product(i, to):
            d = pl.multiple_of(i * STAGE, STAGE)
            t = tan[w, pl.ds(d, STAGE)].reshape(STAGE * own, feat)
            to[...] = dot(t, w_self[...])

        def use(i, a, part, acc):
            for j in range(STAGE):
                d = i * STAGE + j
                m0 = mixed[0, pl.ds(d, 1)]
                m1 = mixed[1, pl.ds(d, 1)]
                ch = a[j * own : (j + 1) * own] + jnp.where(own_up, m0, m1)
                acc = acc + ch * ch
                p = (ch * weighted).reshape(own // 8, 8, feat).sum(axis=0)
                part[8 * j : 8 * j + 8] = p[:, :128] + p[:, 128:]
            for b in range(STAGE // 8):
                r = part[pl.ds(64 * b, 8, stride=8)]
                for k in range(1, 8):
                    r = r + part[pl.ds(64 * b + k, 8, stride=8)]
                partial[pl.ds(pl.multiple_of(i * STAGE + b * 8, 8), 8)] = r
            return acc

        stages = dirs // STAGE

        def step(i, acc):
            product(2 * i + 1, prod_b)
            acc = use(2 * i, prod_a, part_a, acc)
            product(jnp.minimum(2 * i + 2, stages - 1), prod_a)
            return use(2 * i + 1, prod_b, part_b, acc)

        product(0, prod_a)
        squares = lax.fori_loop(0, stages // 2, step, jnp.zeros((own, feat), F32))
        lap = own_slopes * lap_pre_s[w] + own_curve * squares
        lap_out[w] = lap
        lp = (lap * gain).reshape(own // 8, 8, feat).sum(axis=0)
        partial[dirs : dirs + 1] = jnp.sum(lp[:, :128] + lp[:, 128:], axis=0, keepdims=True)
        g = lax.dot_general(
            ones, partial[...], (((1,), (1,)), ((), ())),
            precision=lax.Precision.HIGHEST, preferred_element_type=F32,
        )
        own_ex[...] = jnp.where(iota((8, 256), 0) == w, g, own_ex[...])
        if w == 2:
            scatter_wait(shard_s, recv_s, 0)
            mine_s[...] = add_up(recv_s, XY)
            over_z(mine_s, zs, 0)

    ex = to_partner(own_ex, got_ex, walkers + 2)
    ex.start()
    ex.wait()
    both = own_ex[...] + got_ex[...]
    lane = iota((8, 256), 1)
    both = jnp.where(lane < dirs, both * both, jnp.where(lane == dirs, both, 0.0))
    pot = jnp.zeros((8, 1), F32)
    for w in range(walkers):
        pot = jnp.where(row81 == w, potential[w], pot)
    energy = -0.5 * jnp.sum(both, axis=1, keepdims=True) + pot
    diagonal = iota((8, 128), 0) == iota((8, 128), 1)
    energy_out[...] = jnp.sum(jnp.where(diagonal, energy, 0.0), axis=0, keepdims=True)
    esum = jnp.sum(energy, axis=0, keepdims=True)
    own_e[...] = jnp.broadcast_to(esum, (1, 128))
    scatter(own_e, plane_e, 3, whole=True)
    for c in range(2):
        grad = energy[0:1] * terms[0, :, c]
        for w in range(1, walkers):
            grad = grad + energy[w : w + 1] * terms[w, :, c]
        shard_e[c] = grad
        scatter(shard_e.at[c], recv_e.at[c], 1 + c)
    over_z_wait(mine_s, zs, 0)
    scatter_wait(own_e, plane_e, 3, whole=True)
    mine_z[...] = add_up(plane_e, XY)
    over_z(mine_z, all_e, 3)
    local = mine_z[:, :1] / (walkers * XY)
    for c in range(2):
        scatter_wait(shard_e.at[c], recv_e.at[c], 1 + c)
        mine_e[c] = (add_up(recv_e.at[c], XY) - local * mine_s[c]).astype(BF16)
        over_z(mine_e.at[c], ze.at[c], 1 + c)
    over_z_wait(mine_z, all_e, 3)
    center = add_up(all_e, NZ)[:, :1] / (walkers * XY * NZ)
    rest = jnp.zeros((2, 8, feat), F32)
    for j in range(NZ):
        rest = rest + (all_e[j, :, :1] / (walkers * XY) - center) * zs[j]

    def gather_copy(k, other, matrix, slot, c, i):
        to, _ = across(k)
        return pltpu.make_async_remote_copy(
            src_ref=grads_out.at[core, c, here],
            dst_ref=grads_out.at[matrix, c, slot],
            send_sem=ag_send.at[2 * c + i, k],
            recv_sem=ag_recv.at[2 * c + i, k],
            device_id=(to, other),
            device_id_type=MESH,
        )

    for c in range(2):
        over_z_wait(mine_e.at[c], ze.at[c], 1 + c)
        grad = rest[c]
        for j in range(NZ):
            grad = grad + ze[c, j].astype(F32)
        grads_out[core, c, here] = grad.astype(BF16)
        gather_copy(0, 1 - core, core, here, c, 1).start()
        for k in range(1, XY):
            gather_copy(k, core, core, here, c, 0).start()
            gather_copy(k, 1 - core, core, here, c, 1).start()
    for c in range(2):
        gather_copy(0, 1 - core, 1 - core, here, c, 1).wait()
        for k in range(1, XY):
            gather_copy(k, core, core, behind(k), c, 0).wait()
            gather_copy(k, 1 - core, 1 - core, behind(k), c, 1).wait()


def results(lap, energy, grads, lap_out, energy_out, self_out, spin_out):
    lap_out[...] = lap[...]
    energy_out[...] = energy[0, : energy_out.shape[0]]
    for out, i in ((self_out, 0), (spin_out, 1)):
        halves = [grads[i, c].astype(F32)[:, None] for c in range(2)]
        out[...] = jnp.concatenate(halves, 1).reshape(out.shape)


def shards(
    values, lap_in, tangent, slot_electron, spin_up, w_self, w_spin, bias, readout, potential
):
    walkers, dirs, own, feat = tangent.shape
    elec = slot_electron.shape[1]
    per = feat // XY // 2
    vmem = pl.BlockSpec(memory_space=pltpu.VMEM)
    smem = pl.BlockSpec(memory_space=pltpu.SMEM)
    hbm = pl.BlockSpec(memory_space=pl.ANY)
    dma = pltpu.SemaphoreType.DMA
    lap, energy, grads = pl.pallas_call(
        body,
        out_shape=(
            jax.ShapeDtypeStruct((walkers, own, feat), F32),
            jax.ShapeDtypeStruct((1, 128), F32),
            jax.ShapeDtypeStruct((2, 2, XY, per, feat), BF16),
        ),
        in_specs=[hbm, hbm, hbm, vmem, smem, vmem, vmem, vmem, vmem, smem],
        out_specs=(vmem, vmem, vmem),
        scratch_shapes=[
            pltpu.VMEM((walkers, elec, feat), BF16),
            pltpu.VMEM((walkers, elec, feat), BF16),
            pltpu.VMEM((walkers, dirs, own, feat), BF16),
            pltpu.VMEM((walkers, 2, dirs, feat), F32),
            pltpu.VMEM((walkers, 2, dirs, feat), F32),
            pltpu.VMEM((2, dirs, feat), F32),
            pltpu.VMEM((walkers, 2 * BLOCK, BLOCK * own), BF16),
            pltpu.VMEM((walkers, XY, 2, per, feat), F32),
            pltpu.VMEM((2, walkers, elec, feat), F32),
            pltpu.VMEM((walkers, own, feat), F32),
            pltpu.VMEM((256, 128), F32),
            pltpu.VMEM((STAGE * own, feat), F32),
            pltpu.VMEM((STAGE * own, feat), F32),
            pltpu.VMEM((STAGE * 8, 128), F32),
            pltpu.VMEM((STAGE * 8, 128), F32),
            pltpu.VMEM((8, 256), F32),
            pltpu.VMEM((8, 256), F32),
            pltpu.VMEM((XY, 2, per, feat), F32),
            pltpu.VMEM((XY, 2, per, feat), F32),
            pltpu.VMEM((2, per, feat), F32),
            pltpu.VMEM((NZ, 2, per, feat), F32),
            pltpu.VMEM((2, XY, per, feat), F32),
            pltpu.VMEM((2, XY, per, feat), F32),
            pltpu.VMEM((2, per, feat), BF16),
            pltpu.VMEM((2, NZ, per, feat), BF16),
            pltpu.VMEM((1, 128), F32),
            pltpu.VMEM((XY, 1, 128), F32),
            pltpu.VMEM((1, 128), F32),
            pltpu.VMEM((NZ, 1, 128), F32),
            dma((2,)),
            dma((walkers,)),
            dma((walkers + 3,)),
            dma((walkers + 3,)),
            dma((4, XY)),
            dma((4, XY)),
            dma((4, NZ)),
            dma((4, NZ)),
            dma((4, XY)),
            dma((4, XY)),
        ],
        compiler_params=pltpu.CompilerParams(
            collective_id=0, has_side_effects=True, vmem_limit_bytes=60 << 20
        ),
        name="forward_laplacian",
    )(values, lap_in, tangent, slot_electron, spin_up, w_self, w_spin, bias, readout, potential)
    return pl.pallas_call(
        results,
        out_shape=(
            jax.ShapeDtypeStruct((walkers, own, feat), F32),
            jax.ShapeDtypeStruct((walkers,), F32),
            jax.ShapeDtypeStruct((feat, feat), F32),
            jax.ShapeDtypeStruct((feat, feat), F32),
        ),
        in_specs=[vmem, vmem, vmem],
        out_specs=(vmem, vmem, vmem, vmem),
        name="results",
    )(lap, energy, grads)


def solution(mesh):
    placed = (
        P("walk", "tan", None),
        P("walk", "tan", None),
        P("walk", None, "tan", None),
        P("walk", None),
        P("walk"),
        P(),
        P(),
        P(),
        P(),
        P("walk"),
    )
    return jax.shard_map(
        shards,
        mesh=mesh,
        in_specs=placed,
        out_specs=(P("walk", "tan", None), P("walk"), P(), P()),
        check_vma=False,
    )
```

time: 69.8 us -> 51.6 us (0.74)
  Pallas kernels: 64.3 us -> 50.9 us
  local copies, waits for them, and re-layouts: 4.68 us -> 0 us
    pallas_call x1, Pallas kernels: 64.3 us -> 49 us  [shards(): pl.pallas_call(body, out_shape=(jax.ShapeDtypeStruct((walkers, own, feat)...]
    slice x2 -> x0, local copies, waits for them, and re-layouts: 3.11 us -> none  [shards(): return (lap, energy[:walkers, 0], grads[0], grads[1])]
    pallas_call x0 -> x1, Pallas kernels: none -> 1.87 us  [shards(): pl.pallas_call(results, out_shape=(jax.ShapeDtypeStruct((walkers, own, fe...]
    unnamed x1 -> x0, local copies, waits for them, and re-layouts: 1.57 us -> none
where the time goes in v2:
time: 51.6 us; the launch traced here: 51.5 us
  Pallas kernels  50.9 us (99%)
  between operations  0.64 us (1%)
    pallas_call x1, Pallas kernels, shards(): pl.pallas_call(body, out_shape=(jax.ShapeDtypeStruct((walkers, own, feat)...  49 us
    pallas_call x1, Pallas kernels, shards(): pl.pallas_call(results, out_shape=(jax.ShapeDtypeStruct((walkers, own, fe...  1.87 us

profile of v2, /device:TPU:1, one launch (start us, length us, event | category | flops | bytes accessed | tf_op | source)
XLA Modules:
  0.0 51.5 jit_solution(3962629599150802774)
XLA Ops:
  0.6 49.0 %forward_laplacian.1 = (f32[4,32,256]{2,1,0:T(8,128)}, f32[1,128]{1,0:T(1,128)}, bf16[2,2,16,8,256]{4,3,2,1,0:T(8,128)(2,1)}) custom-call(bf16[4,32,256]{2,1,0:T(8,128)(2,1)} %values.1, bf16[4,32,256]{2,1,0:T(8,128)(2,1)} %lap_in.1, bf16[4,192,32,256]{3,2,1,0:T(8,128)(2,1)} %tangent.1, s32[4,64]{1,0:T(4,128)} %slots.1, s32[4]{0:T(128)} %spin.1, ...), custom_call_target="tpu_custom_call" | custom-call | tf_op jit(solution)/shard_map/forward_laplacian/pallas_call | solution.py:394
  49.7 1.9 %results.1 = (f32[4,32,256]{2,1,0:T(8,128)}, f32[4]{0:T(128)}, f32[256,256]{1,0:T(8,128)}, f32[256,256]{1,0:T(8,128)}) custom-call(f32[4,32,256]{2,1,0:T(8,128)} %get-tuple-element.7.lap, f32[1,128]{1,0:T(1,128)} %get-tuple-element.8.energy, bf16[2,2,16,8,256]{4,3,2,1,0:T(8,128)(2,1)} %get-tuple-element.9.grads), custom_call_target="tpu_custom_call" | custom-call | tf_op jit(solution)/shard_map/results/pallas_call | solution.py:449

commit v3 on v2

--- a/solution.py
+++ b/solution.py
@@ -10,6 +10,8 @@
 BF16 = jnp.bfloat16
 NX, NZ, NY = 4, 8, 4
 XY = NX * NY
+FAR_XY = (10, 6, 9, 11, 14, 2, 8, 5, 7, 13, 15, 1, 3, 4, 12)
+FAR_Z = (4, 3, 5, 2, 6, 1, 7)
 BLOCK = 8
 STAGE = 32
 
@@ -23,16 +25,17 @@
 
 
 def body(
-    values, lap_in, tangent, slots, spin, w_self, w_spin, bias, readout, potential,
+    values, lap_in, tangent, slots_in, spin, w_self_in, w_spin_in, bias_in, readout_in, potential,
     lap_out, energy_out, grads_out,
     full_v, full_l, tan, own_sums, got_sums, mixed, sel, terms, slopes_s, lap_pre_s,
     partial, prod_a, prod_b, part_a, part_b, own_ex, got_ex, shard_s, recv_s, mine_s, zs, shard_e, recv_e, mine_e, ze,
     own_e, plane_e, mine_z, all_e,
+    slots, w_self, w_spin, bias, readout,
     load_sem, tan_sem, pair_send, pair_recv,
     rs_send, rs_recv, z_send, z_recv, ag_send, ag_recv,
 ):
     walkers, dirs, own, feat = tangent.shape
-    elec = slots.shape[1]
+    elec = slots_in.shape[1]
     rows = BLOCK * own
     blocks = dirs // BLOCK
     me = lax.axis_index("walk")
@@ -59,23 +62,36 @@
     off = pl.multiple_of(core * own, own)
     load_v = pltpu.make_async_copy(values, full_v.at[:, pl.ds(off, own)], load_sem.at[0])
     load_l = pltpu.make_async_copy(lap_in, full_l.at[:, pl.ds(off, own)], load_sem.at[1])
+    small = [
+        pltpu.make_async_copy(src, dst, load_sem.at[2 + i])
+        for i, (src, dst) in enumerate(
+            (
+                (slots_in, slots),
+                (w_self_in, w_self),
+                (w_spin_in, w_spin),
+                (bias_in, bias),
+                (readout_in, readout),
+            )
+        )
+    ]
+    small[0].start()
     for w in range(walkers):
         pltpu.make_async_copy(tangent.at[w], tan.at[w], tan_sem.at[w]).start()
         if w == 0:
             load_v.start()
             load_l.start()
+            for copy in small[1:]:
+                copy.start()
 
     barrier = pltpu.get_barrier_semaphore()
     pl.semaphore_signal(barrier, inc=1, device_id=partner, device_id_type=MESH)
 
     for k in range(1, XY):
-        for other in (core, 1 - core):
-            pl.semaphore_signal(
-                barrier, inc=1, device_id=(across(k)[0], other), device_id_type=MESH
-            )
+        pl.semaphore_signal(barrier, inc=1, device_id=(across(k)[0], core), device_id_type=MESH)
     for k in range(1, NZ):
         pl.semaphore_signal(barrier, inc=1, device_id=(along(k), core), device_id_type=MESH)
 
+    small[0].wait()
     s8 = jnp.concatenate([slots[...]] * (8 // walkers), 0)
     r8 = iota((8, elec), 0) % walkers
     n8 = jnp.zeros((8, elec), jnp.int32)
@@ -123,10 +139,11 @@
     def tan_wait(w):
         pltpu.make_async_copy(tangent.at[w], tan.at[w], tan_sem.at[w]).wait()
 
-    ahead = 2
-    tan_wait(0)
-    group_sums(0)
-    pl.semaphore_wait(barrier, 1 + 2 * (XY - 1) + NZ - 1)
+    ahead = 3
+    for w in range(2):
+        tan_wait(w)
+        group_sums(w)
+    pl.semaphore_wait(barrier, 1 + (XY - 1) + NZ - 1)
 
     def to_partner(src, dst, i):
         return pltpu.make_async_remote_copy(
@@ -143,10 +160,13 @@
     send_v.start()
     send_l.start()
     sums_copy(0).start()
-    for w in range(1, ahead):
+    sums_copy(1).start()
+    for w in range(2, ahead):
         tan_wait(w)
         group_sums(w)
         sums_copy(w).start()
+    for copy in small[1:]:
+        copy.wait()
     load_v.wait()
     load_l.wait()
     send_v.wait()
@@ -190,7 +210,7 @@
     def scatter(src, dst, i, whole=False):
         dst[here] = src[...] if whole else src[here]
 
-        for k in range(1, XY):
+        for k in FAR_XY:
             to, slot = across(k)
             pltpu.make_async_remote_copy(
                 src_ref=src if whole else src.at[slot],
@@ -202,7 +222,7 @@
             ).start()
 
     def scatter_wait(src, dst, i, whole=False):
-        for k in range(1, XY):
+        for k in FAR_XY:
             to, slot = across(k)
             pltpu.make_async_remote_copy(
                 src_ref=src if whole else src.at[slot],
@@ -215,7 +235,7 @@
 
     def over_z(src, dst, i):
         dst[z] = src[...]
-        for k in range(1, NZ):
+        for k in FAR_Z:
             pltpu.make_async_remote_copy(
                 src_ref=src,
                 dst_ref=dst.at[z],
@@ -226,7 +246,7 @@
             ).start()
 
     def over_z_wait(src, dst, i):
-        for k in range(1, NZ):
+        for k in FAR_Z:
             pltpu.make_async_remote_copy(
                 src_ref=src,
                 dst_ref=dst.at[lax.rem(z - k + NZ, NZ)],
@@ -304,13 +324,11 @@
             precision=lax.Precision.HIGHEST, preferred_element_type=F32,
         )
         own_ex[...] = jnp.where(iota((8, 256), 0) == w, g, own_ex[...])
-        if w == 2:
-            scatter_wait(shard_s, recv_s, 0)
-            mine_s[...] = add_up(recv_s, XY)
-            over_z(mine_s, zs, 0)
-
     ex = to_partner(own_ex, got_ex, walkers + 2)
     ex.start()
+    scatter_wait(shard_s, recv_s, 0)
+    mine_s[...] = add_up(recv_s, XY)
+    over_z(mine_s, zs, 0)
     ex.wait()
     both = own_ex[...] + got_ex[...]
     lane = iota((8, 256), 1)
@@ -330,7 +348,6 @@
             grad = grad + energy[w : w + 1] * terms[w, :, c]
         shard_e[c] = grad
         scatter(shard_e.at[c], recv_e.at[c], 1 + c)
-    over_z_wait(mine_s, zs, 0)
     scatter_wait(own_e, plane_e, 3, whole=True)
     mine_z[...] = add_up(plane_e, XY)
     over_z(mine_z, all_e, 3)
@@ -339,20 +356,30 @@
         scatter_wait(shard_e.at[c], recv_e.at[c], 1 + c)
         mine_e[c] = (add_up(recv_e.at[c], XY) - local * mine_s[c]).astype(BF16)
         over_z(mine_e.at[c], ze.at[c], 1 + c)
+    over_z_wait(mine_s, zs, 0)
     over_z_wait(mine_z, all_e, 3)
     center = add_up(all_e, NZ)[:, :1] / (walkers * XY * NZ)
     rest = jnp.zeros((2, 8, feat), F32)
     for j in range(NZ):
         rest = rest + (all_e[j, :, :1] / (walkers * XY) - center) * zs[j]
 
-    def gather_copy(k, other, matrix, slot, c, i):
-        to, _ = across(k)
+    def gather_copy(k, slot, c):
         return pltpu.make_async_remote_copy(
             src_ref=grads_out.at[core, c, here],
-            dst_ref=grads_out.at[matrix, c, slot],
-            send_sem=ag_send.at[2 * c + i, k],
-            recv_sem=ag_recv.at[2 * c + i, k],
-            device_id=(to, other),
+            dst_ref=grads_out.at[core, c, slot],
+            send_sem=ag_send.at[c, k],
+            recv_sem=ag_recv.at[c, k],
+            device_id=(across(k)[0], core),
+            device_id_type=MESH,
+        )
+
+    def hand_over(matrix, c):
+        return pltpu.make_async_remote_copy(
+            src_ref=grads_out.at[core, c],
+            dst_ref=grads_out.at[matrix, c],
+            send_sem=ag_send.at[c, 0],
+            recv_sem=ag_recv.at[c, 0],
+            device_id=partner,
             device_id_type=MESH,
         )
 
@@ -362,15 +389,14 @@
         for j in range(NZ):
             grad = grad + ze[c, j].astype(F32)
         grads_out[core, c, here] = grad.astype(BF16)
-        gather_copy(0, 1 - core, core, here, c, 1).start()
-        for k in range(1, XY):
-            gather_copy(k, core, core, here, c, 0).start()
-            gather_copy(k, 1 - core, core, here, c, 1).start()
+        for k in FAR_XY:
+            gather_copy(k, here, c).start()
     for c in range(2):
-        gather_copy(0, 1 - core, 1 - core, here, c, 1).wait()
-        for k in range(1, XY):
-            gather_copy(k, core, core, behind(k), c, 0).wait()
-            gather_copy(k, 1 - core, 1 - core, behind(k), c, 1).wait()
+        for k in FAR_XY:
+            gather_copy(k, behind(k), c).wait()
+        hand_over(core, c).start()
+    for c in range(2):
+        hand_over(1 - core, c).wait()
 
 
 def results(lap, energy, grads, lap_out, energy_out, self_out, spin_out):
@@ -398,7 +424,7 @@
             jax.ShapeDtypeStruct((1, 128), F32),
             jax.ShapeDtypeStruct((2, 2, XY, per, feat), BF16),
         ),
-        in_specs=[hbm, hbm, hbm, vmem, smem, vmem, vmem, vmem, vmem, smem],
+        in_specs=[hbm, hbm, hbm, hbm, smem, hbm, hbm, hbm, hbm, smem],
         out_specs=(vmem, vmem, vmem),
         scratch_shapes=[
             pltpu.VMEM((walkers, elec, feat), BF16),
@@ -430,7 +456,12 @@
             pltpu.VMEM((XY, 1, 128), F32),
             pltpu.VMEM((1, 128), F32),
             pltpu.VMEM((NZ, 1, 128), F32),
-            dma((2,)),
+            pltpu.VMEM((walkers, elec), jnp.int32),
+            pltpu.VMEM((feat, feat), BF16),
+            pltpu.VMEM((feat, feat), BF16),
+            pltpu.VMEM((feat,), F32),
+            pltpu.VMEM((feat,), F32),
+            dma((7,)),
             dma((walkers,)),
             dma((walkers + 3,)),
             dma((walkers + 3,)),
@@ -438,8 +469,8 @@
             dma((4, XY)),
             dma((4, NZ)),
             dma((4, NZ)),
-            dma((4, XY)),
-            dma((4, XY)),
+            dma((2, XY)),
+            dma((2, XY)),
         ],
         compiler_params=pltpu.CompilerParams(
             collective_id=0, has_side_effects=True, vmem_limit_bytes=60 << 20

time: 51.6 us -> 50.1 us (0.971)
  Pallas kernels: 50.9 us -> 49.4 us
    pallas_call x1, Pallas kernels: 49 us -> 47.5 us  [shards(): pl.pallas_call(body, out_shape=(jax.ShapeDtypeStruct((walkers, own, feat)...]
where the time goes in v3:
time: 50.1 us; the launch traced here: 50 us
  Pallas kernels  49.4 us (99%)
  between operations  0.64 us (1%)
    pallas_call x1, Pallas kernels, shards(): pl.pallas_call(body, out_shape=(jax.ShapeDtypeStruct((walkers, own, feat)...  47.5 us
    pallas_call x1, Pallas kernels, shards(): pl.pallas_call(results, out_shape=(jax.ShapeDtypeStruct((walkers, own, fe...  1.87 us

profile of v3, /device:TPU:1, one launch (start us, length us, event | category | flops | bytes accessed | tf_op | source)
XLA Modules:
  0.0 50.0 jit_solution(4680971591227161306)
XLA Ops:
  0.6 47.5 %forward_laplacian.1 = (f32[4,32,256]{2,1,0:T(8,128)}, f32[1,128]{1,0:T(1,128)}, bf16[2,2,16,8,256]{4,3,2,1,0:T(8,128)(2,1)}) custom-call(bf16[4,32,256]{2,1,0:T(8,128)(2,1)} %values.1, bf16[4,32,256]{2,1,0:T(8,128)(2,1)} %lap_in.1, bf16[4,192,32,256]{3,2,1,0:T(8,128)(2,1)} %tangent.1, s32[4,64]{1,0:T(4,128)} %slots_in.1, s32[4]{0:T(128)} %spin.1, ...), custom_call_target="tpu_custom_call" | custom-call | tf_op jit(solution)/shard_map/forward_laplacian/pallas_call | solution.py:420
  48.1 1.9 %results.1 = (f32[4,32,256]{2,1,0:T(8,128)}, f32[4]{0:T(128)}, f32[256,256]{1,0:T(8,128)}, f32[256,256]{1,0:T(8,128)}) custom-call(f32[4,32,256]{2,1,0:T(8,128)} %get-tuple-element.7.lap, f32[1,128]{1,0:T(1,128)} %get-tuple-element.8.energy, bf16[2,2,16,8,256]{4,3,2,1,0:T(8,128)(2,1)} %get-tuple-element.9.grads), custom_call_target="tpu_custom_call" | custom-call | tf_op jit(solution)/shard_map/results/pallas_call | solution.py:480

commit v4 on v3

--- a/solution.py
+++ b/solution.py
@@ -440,8 +440,8 @@
             pltpu.VMEM((256, 128), F32),
             pltpu.VMEM((STAGE * own, feat), F32),
             pltpu.VMEM((STAGE * own, feat), F32),
-            pltpu.VMEM((STAGE * 8, 128), F32),
-            pltpu.VMEM((STAGE * 8, 128), F32),
+            pltpu.VMEM((STAGE * 8 + 8, 128), F32),
+            pltpu.VMEM((STAGE * 8 + 8, 128), F32),
             pltpu.VMEM((8, 256), F32),
             pltpu.VMEM((8, 256), F32),
             pltpu.VMEM((XY, 2, per, feat), F32),

time: 50.1 us -> 50.1 us (level)
  no operation moved by 1% of the time
where the time goes in v4:
time: 50.1 us; the launch traced here: 50 us
  Pallas kernels  49.4 us (99%)
  between operations  0.64 us (1%)
    pallas_call x1, Pallas kernels, shards(): pl.pallas_call(body, out_shape=(jax.ShapeDtypeStruct((walkers, own, feat)...  47.5 us
    pallas_call x1, Pallas kernels, shards(): pl.pallas_call(results, out_shape=(jax.ShapeDtypeStruct((walkers, own, fe...  1.87 us

profile of v4, /device:TPU:1, one launch (start us, length us, event | category | flops | bytes accessed | tf_op | source)
XLA Modules:
  0.0 50.0 jit_solution(2101528972748544425)
XLA Ops:
  0.6 47.5 %forward_laplacian.1 = (f32[4,32,256]{2,1,0:T(8,128)}, f32[1,128]{1,0:T(1,128)}, bf16[2,2,16,8,256]{4,3,2,1,0:T(8,128)(2,1)}) custom-call(bf16[4,32,256]{2,1,0:T(8,128)(2,1)} %values.1, bf16[4,32,256]{2,1,0:T(8,128)(2,1)} %lap_in.1, bf16[4,192,32,256]{3,2,1,0:T(8,128)(2,1)} %tangent.1, s32[4,64]{1,0:T(4,128)} %slots_in.1, s32[4]{0:T(128)} %spin.1, ...), custom_call_target="tpu_custom_call" | custom-call | tf_op jit(solution)/shard_map/forward_laplacian/pallas_call | solution.py:420
  48.1 1.9 %results.1 = (f32[4,32,256]{2,1,0:T(8,128)}, f32[4]{0:T(128)}, f32[256,256]{1,0:T(8,128)}, f32[256,256]{1,0:T(8,128)}) custom-call(f32[4,32,256]{2,1,0:T(8,128)} %get-tuple-element.7.lap, f32[1,128]{1,0:T(1,128)} %get-tuple-element.8.energy, bf16[2,2,16,8,256]{4,3,2,1,0:T(8,128)(2,1)} %get-tuple-element.9.grads), custom_call_target="tpu_custom_call" | custom-call | tf_op jit(solution)/shard_map/results/pallas_call | solution.py:480
